TPU v7x, 32 devices: a whole 2x2x4 slice. The times are simulated.
32 devices in a mesh: dp: 8 (over y, x, core), tensor: 4 (over z).
Axes of the slice: x: 2, y: 2, z: 4, core: 2. Of those that a mesh axis runs over, the one named last changes fastest.
Arguments:
- queries: bfloat16 [2048, 3072], P('dp', 'tensor'), may hold values from -96 to 96
- keys: bfloat16 [2048, 512], P('dp'), may hold values from -6 to 6
- values: bfloat16 [2048, 512], P('dp'), may hold values from -6 to 6
- lengths: int32 [4], replicated, may hold values from 1 to 1536, 2048 in all
- assignment: int32 [8, 8], replicated, may hold values from 0 to 7, each once within a row
- out_weight: bfloat16 [3072, 6144], P('tensor'), may hold values from -0.109375 to 0.109375
Outputs:
- mixed: bfloat16 [2048, 6144], P(('dp', 'tensor'))
Inputs may be any that keep to these rules, and one draw needn't show every extreme that they name: `lengths`: the prompts fill the 2048 positions in order, one of them exactly 1536 long. `assignment`: each row is a permutation of 0 to 7.
All inputs are finite; a program needn't handle non-finite values.
Results may differ from a plain program's by a relative error of at most 0.014.
Values may be sent and summed in bfloat16 or wider, within the bound.
A program may use at most 64 MiB of HBM per device.

v0:
```python
import jax
import jax.numpy as jnp
from jax import lax
from jax.sharding import PartitionSpec as P

HD = 128
HEADS = 24
KV_HEADS = 4


def local(queries, keys, values, lengths, assignment, out_weight):
    n_groups = lax.axis_size("dp")
    my_group = lax.axis_index("dp")
    my_lane = lax.axis_index("tensor")
    tok_rows = queries.shape[0]
    q_width = queries.shape[1]
    heads_here = q_width // HD
    piece_rows = tok_rows // n_groups
    all_rows = tok_rows * n_groups
    score_scale = HD ** (-0.5)
    kv_head = my_lane * heads_here // (HEADS // KV_HEADS)
    own_keys = lax.dynamic_slice_in_dim(keys, kv_head * HD, HD, 1)
    own_values = lax.dynamic_slice_in_dim(values, kv_head * HD, HD, 1)
    doc_ends = jnp.cumsum(lengths)
    places = jnp.arange(all_rows, dtype=jnp.int32)
    doc_all = jnp.sum((places[:, None] >= doc_ends[None, :]).astype(jnp.int32), axis=1)

    def attend(softmax_state, query_rows, q_pos, q_doc, k_rows, v_rows, k_first):
        k_pos = k_first + jnp.arange(k_rows.shape[0], dtype=jnp.int32)
        k_doc = doc_all[jnp.clip(k_pos, 0, all_rows - 1)]
        visible = (
            (k_doc[None, :] == q_doc[:, None])
            & (k_pos[None, :] <= q_pos[:, None])
            & (k_pos >= 0)[None, :]
        )

        def compute(inner_state):
            running, totals, weighted = inner_state
            scores = (
                jnp.einsum("qhd,kd->hqk", query_rows, k_rows, preferred_element_type=jnp.float32)
                * score_scale
            )
            scores = jnp.where(visible[None], scores, -1e30)
            highest = jnp.maximum(running, jnp.max(scores, axis=2))
            rescale = jnp.exp(running - highest)
            weights = jnp.exp(scores - highest[:, :, None]) * visible[None].astype(jnp.float32)
            totals = rescale * totals + jnp.sum(weights, axis=2)
            weighted = weighted * jnp.transpose(rescale)[:, :, None] + jnp.einsum(
                "hqk,kd->qhd",
                weights.astype(jnp.bfloat16),
                v_rows,
                preferred_element_type=jnp.float32,
            )
            return (highest, totals, weighted)

        def keep(inner_state):
            return inner_state

        return lax.cond(jnp.any(visible), compute, keep, softmax_state)

    outgoing = queries.reshape(n_groups, piece_rows, q_width)[assignment[my_group]]
    arrived = lax.all_to_all(outgoing, "dp", split_axis=0, concat_axis=0, tiled=True)
    offsets = assignment[:, my_group]
    q_pos = (
        jnp.arange(n_groups, dtype=jnp.int32)[:, None] * tok_rows
        + offsets[:, None] * piece_rows
        + jnp.arange(piece_rows, dtype=jnp.int32)[None, :]
    ).reshape(tok_rows)
    query_rows = arrived.reshape(tok_rows, heads_here, HD)
    q_doc = doc_all[q_pos]
    running = jnp.full((heads_here, tok_rows), -1e30, jnp.float32)
    totals = jnp.zeros((heads_here, tok_rows), jnp.float32)
    weighted = jnp.zeros((tok_rows, heads_here, HD), jnp.float32)
    k_rows = lax.all_gather(own_keys, "dp", axis=0, tiled=True)
    v_rows = lax.all_gather(own_values, "dp", axis=0, tiled=True)
    row_count = k_rows.shape[0]
    block_count = max(row_count // tok_rows, 1)
    block_rows = row_count // block_count

    def one_step(block_index, inner_state):
        k_block = lax.dynamic_slice_in_dim(k_rows, block_index * block_rows, block_rows, 0)
        v_block = lax.dynamic_slice_in_dim(v_rows, block_index * block_rows, block_rows, 0)
        return attend(
            inner_state, query_rows, q_pos, q_doc, k_block, v_block, block_index * block_rows
        )

    softmax_state = lax.fori_loop(0, block_count, one_step, (running, totals, weighted))
    running, totals, weighted = softmax_state
    attended = (
        (weighted / jnp.transpose(totals)[:, :, None])
        .reshape(tok_rows, q_width)
        .astype(jnp.bfloat16)
    )
    return lax.psum_scatter(
        jnp.dot(attended, out_weight, preferred_element_type=jnp.float32).astype(jnp.bfloat16),
        "tensor",
        scatter_dimension=0,
        tiled=True,
    )


def solution(mesh):
    in_specs = (P("dp", "tensor"), P("dp", None), P("dp", None), P(), P(), P("tensor", None))
    out_specs = P(("dp", "tensor"), None)
    return jax.shard_map(local, mesh=mesh, in_specs=in_specs, out_specs=out_specs, check_vma=False)
```

profile of v0, /device:TPU:8, one launch (start us, length us, event | category | flops | bytes accessed | tf_op | source)
XLA Modules:
  0.0 152.8 jit_solution(18272616244616208686)
XLA Ops:
  7.5 1.3 gather_fusion.2
  8.9 3.7 %all-to-all-start = ((bf16[8,32,768]{2,1,0:T(8,128)(2,1)}), bf16[8,32,768]{2,1,0:T(8,128)(2,1)S(1)}, u32[]{:S(2)}, u32[]{:S(2)}) async-start(bf16[8,32,768]{2,1,0:T(8,128)(2,1)} %gather_fusion.2), calls=%async_computation | async-start | bytes 786432 | tf_op jit(solution)/shard_map/all_to_all | solution.py:62
  14.2 1.7 %gather_fusion.1 = s32[256]{0:T(256)S(1)} fusion(s32[2048]{0:T(1024)S(1)} %convert_reduce_fusion, s32[1024]{0:T(1024)S(1)} %pad_clamp_fusion.2), kind=kCustom, calls=%fused_computation.1 | custom fusion | bytes 3072 | tf_op jit(solution)/shard_map/gather | solution.py:70
  16.7 10.3 %all_gather.6 = bf16[2048,128]{1,0:T(8,128)(2,1)S(1)} all-gather(bf16[256,128]{1,0:T(8,128)(2,1)S(1)} %constant_dynamic-slice_fusion.2), channel_id=1, replica_groups=mesh['dp'=8,'tensor'=4] {'dp'}, dimensions={0}, use_global_device_ids=true | all-gather | bytes 589824 | tf_op jit(solution)/shard_map/all_gather | solution.py:74
  27.0 9.8 %all_gather.7 = bf16[2048,128]{1,0:T(8,128)(2,1)S(1)} all-gather(bf16[256,128]{1,0:T(8,128)(2,1)S(1)} %constant_dynamic-slice_fusion), channel_id=1, replica_groups=mesh['dp'=8,'tensor'=4] {'dp'}, dimensions={0}, use_global_device_ids=true | all-gather | bytes 589824 | tf_op jit(solution)/shard_map/all_gather | solution.py:75
  37.4 40.2 %while.18 = (s32[]{:T(128)}, f32[6,256]{1,0:T(8,128)S(1)}, f32[6,256]{1,0:T(8,128)S(1)}, f32[256,6,128]{2,0,1:T(8,128)S(1)}, s32[2048]{0:T(1024)S(1)}, /*index=5...) while((s32[]{:T(128)}, f32[6,256]{1,0:T(8,128)S(1)}, ...), condition=%wide.region_8.9_spmd.clone, body=%wide.region_2.8_spmd.clone.sunk | while | flops 205659904 | bytes 7919445 | solution.py:87
  37.5 1.7 %gather_fusion = s32[256]{0:T(256)S(1)} fusion(s32[2048]{0:T(1024)S(1)} %get-tuple-element.441, s32[1024]{0:T(1024)S(1)} %pad_clamp_fusion.4), kind=kCustom, calls=%fused_computation.clone.clone.1 | custom fusion | bytes 3072 | tf_op jit(solution)/shard_map/while/body/eval_jaxpr/gather | solution.py:30
  41.0 1.5 conditional.3
  42.5 1.7 %gather_fusion = s32[256]{0:T(256)S(1)} fusion(s32[2048]{0:T(1024)S(1)} %get-tuple-element.441, s32[1024]{0:T(1024)S(1)} %pad_clamp_fusion.4), kind=kCustom, calls=%fused_computation.clone.clone.1 | custom fusion | bytes 3072 | tf_op jit(solution)/shard_map/while/body/eval_jaxpr/gather | solution.py:30
  46.0 1.5 conditional.3
  47.5 1.7 %gather_fusion = s32[256]{0:T(256)S(1)} fusion(s32[2048]{0:T(1024)S(1)} %get-tuple-element.441, s32[1024]{0:T(1024)S(1)} %pad_clamp_fusion.4), kind=kCustom, calls=%fused_computation.clone.clone.1 | custom fusion | bytes 3072 | tf_op jit(solution)/shard_map/while/body/eval_jaxpr/gather | solution.py:30
  51.0 1.5 conditional.3
  52.5 1.7 %gather_fusion = s32[256]{0:T(256)S(1)} fusion(s32[2048]{0:T(1024)S(1)} %get-tuple-element.441, s32[1024]{0:T(1024)S(1)} %pad_clamp_fusion.4), kind=kCustom, calls=%fused_computation.clone.clone.1 | custom fusion | bytes 3072 | tf_op jit(solution)/shard_map/while/body/eval_jaxpr/gather | solution.py:30
  56.0 1.5 conditional.3
  57.6 1.7 %gather_fusion = s32[256]{0:T(256)S(1)} fusion(s32[2048]{0:T(1024)S(1)} %get-tuple-element.441, s32[1024]{0:T(1024)S(1)} %pad_clamp_fusion.4), kind=kCustom, calls=%fused_computation.clone.clone.1 | custom fusion | bytes 3072 | tf_op jit(solution)/shard_map/while/body/eval_jaxpr/gather | solution.py:30
  61.1 1.5 conditional.3
  62.6 1.7 %gather_fusion = s32[256]{0:T(256)S(1)} fusion(s32[2048]{0:T(1024)S(1)} %get-tuple-element.441, s32[1024]{0:T(1024)S(1)} %pad_clamp_fusion.4), kind=kCustom, calls=%fused_computation.clone.clone.1 | custom fusion | bytes 3072 | tf_op jit(solution)/shard_map/while/body/eval_jaxpr/gather | solution.py:30
  66.1 1.5 conditional.3
  67.6 1.7 %gather_fusion = s32[256]{0:T(256)S(1)} fusion(s32[2048]{0:T(1024)S(1)} %get-tuple-element.441, s32[1024]{0:T(1024)S(1)} %pad_clamp_fusion.4), kind=kCustom, calls=%fused_computation.clone.clone.1 | custom fusion | bytes 3072 | tf_op jit(solution)/shard_map/while/body/eval_jaxpr/gather | solution.py:30
  71.1 1.5 conditional.3
  72.7 1.7 %gather_fusion = s32[256]{0:T(256)S(1)} fusion(s32[2048]{0:T(1024)S(1)} %get-tuple-element.441, s32[1024]{0:T(1024)S(1)} %pad_clamp_fusion.4), kind=kCustom, calls=%fused_computation.clone.clone.1 | custom fusion | bytes 3072 | tf_op jit(solution)/shard_map/while/body/eval_jaxpr/gather | solution.py:30
  76.1 1.5 conditional.3
  78.0 7.8 %convolution_convert_fusion = bf16[256,6144]{1,0:T(8,128)(2,1)} fusion(bf16[256,768]{0,1:T(8,128)(2,1)S(1)} %bitcast.37, bf16[768,6144]{1,0:T(8,128)(2,1)} %param.15), kind=kOutput, calls=%fused_computation.27 | convolution fusion | flops 2417491968 | bytes 12976128 | tf_op jit(solution)/shard_map/dot_general | solution.py:95
  85.8 60.1 %reduce-scatter.2.cloned.1.call-done = bf16[64,6144]{1,0:T(8,128)(2,1)} async-done(((bf16[256,6144]{1,0:T(8,128)(2,1)}), bf16[64,6144]{1,0:T(8,128)(2,1)}) %reduce-scatter.2.cloned.1.call-update) | async-done | bytes 786448 | tf_op jit(solution)/shard_map/reduce_scatter | solution.py:94
  (139 shorter events, 24.1 us)
Async XLA Ops:
  6.5 1.0 copy-start
  6.5 6.1 %copy-start.1 = (s32[8,8]{1,0:T(8,128)S(1)}, s32[8,8]{1,0:T(8,128)}, u32[]{:S(2)}) copy-start(s32[8,8]{1,0:T(8,128)} %param.14) | copy-start | bytes 772
  6.5 6.5 %copy-start.2 = (s32[4]{0:T(128)S(1)}, s32[4]{0:T(128)}, u32[]{:S(2)}) copy-start(s32[4]{0:T(128)} %param.13) | copy-start | bytes 52
  8.9 28.0 %all-to-all-start = ((bf16[8,32,768]{2,1,0:T(8,128)(2,1)}), bf16[8,32,768]{2,1,0:T(8,128)(2,1)S(1)}, u32[]{:S(2)}, u32[]{:S(2)}) async-start(bf16[8,32,768]{2,1,0:T(8,128)(2,1)} %gather_fusion.2), calls=%async_computation | async-start | bytes 786432 | tf_op jit(solution)/shard_map/all_to_all | solution.py:62
  12.6 133.3 %reduce-scatter.2.cloned.1.call-start = ((), (), s32[]{:S(2)}) async-start(), calls=%async_computation.2 | async-start | bytes 3932160 | tf_op jit(solution)/shard_map/reduce_scatter | solution.py:94
Sparse Core Ops, SparseCore 0:
  85.9 59.9 reduce-scatter.1
where the time goes:
time: 155 us; the launch traced here: 153 us
  waiting for transfers between devices  60.2 us (39%)
  local copies, waits for them, and re-layouts  20.3 us (13%)
  blocking collectives  20.1 us (13%)
  matrix products  16.5 us (11%)
  between operations  13.5 us (9%)
  other arithmetic  11.7 us (8%)
  loops' own time  6.67 us (4%)
  starting transfers between devices  3.76 us (2%)
    reduce_scatter x1, waiting for transfers between devices, local(): lax.psum_scatter(jnp.dot(attended, out_weight, preferred_element_type=jnp...  60.1 us
    gather x8, local copies, waits for them, and re-layouts, attend(): k_doc = doc_all[jnp.clip(k_pos, 0, all_rows - 1)]  13.8 us
    all_gather x1, blocking collectives, local(): k_rows = lax.all_gather(own_keys, 'dp', axis=0, tiled=True)  10.3 us
    all_gather x1, blocking collectives, local(): v_rows = lax.all_gather(own_values, 'dp', axis=0, tiled=True)  9.79 us
    dot_general x1, matrix products, local(): jnp.dot(attended, out_weight, preferred_element_type=jnp.float32)  7.77 us
    reduce_or x8, other arithmetic, attend(): return lax.cond(jnp.any(visible), compute, keep, softmax_state)  7.09 us
    another operation x1, loops' own time, local(): lax.fori_loop(0, block_count, one_step, (running, totals, weighted))  6.07 us
    dot_general x8, matrix products, compute(): jnp.einsum('hqk,kd->qhd', weights.astype(jnp.bfloat16), v_rows, preferred...  5.6 us
  transfers between devices with their start and end apart: 2, of which 1 were waited for; matrix products, arithmetic and copies ran while one was open for 3% of the time, Pallas kernels for 0%

commit v1 on v0

v1 whole, which is shorter than its diff:
```python
import math

import jax
import jax.numpy as jnp
from jax import lax
from jax.experimental import pallas as pl
from jax.experimental.pallas import tpu as pltpu
from jax.sharding import PartitionSpec as P

HD = 128
HEADS = 24
KV_HEADS = 4
MESH = pl.DeviceIdType.MESH
CHUNKS = 8


def kernel(
    G, T, lengths, assignment, q_hbm, k_hbm, v_hbm, w_hbm, out_ref,
    q_all, q_stage, q_buf, k_buf, v_buf, w_buf, att, in_r, in_l, out_r, out_l,
    load_sem, w_sem, own_sem, k_send, k_recv, v_send, v_recv, q_send, q_recv,
    r_send, r_recv, l_send, l_recv,
):
    me = lax.axis_index("dp")
    z = lax.axis_index("tensor")
    tok_rows, q_width = q_all.shape
    heads_here = q_width // HD
    piece = tok_rows // G
    per_dest = G // T
    out_rows = tok_rows // T
    n_cols = w_buf.shape[1]
    cw = n_cols // CHUNKS
    kv_head = z * heads_here // (HEADS // KV_HEADS)
    kv_cols = pl.ds(pl.multiple_of(kv_head * HD, HD), HD)

    load_q = pltpu.make_async_copy(q_hbm, q_all, load_sem)
    load_q.start()
    barrier = pltpu.get_barrier_semaphore()
    for i in range(1, G):
        pl.semaphore_signal(
            barrier, inc=1, device_id=(lax.rem(me + i, G), z), device_id_type=MESH
        )
    for i in range(1, T):
        pl.semaphore_signal(
            barrier, inc=1, device_id=(me, lax.rem(z + i, T)), device_id_type=MESH
        )
    own_k = pltpu.make_async_copy(k_hbm.at[:, kv_cols], k_buf.at[me], own_sem.at[0])
    own_v = pltpu.make_async_copy(v_hbm.at[:, kv_cols], v_buf.at[me], own_sem.at[1])
    own_k.start()
    own_v.start()
    load_w = pltpu.make_async_copy(w_hbm, w_buf, w_sem)
    load_w.start()
    load_q.wait()
    place = lax.broadcasted_iota(jnp.int32, (tok_rows, 1), 0)
    source_row = jnp.zeros((tok_rows, 1), jnp.int32)
    for g in range(G):
        here = (place >= g * piece) & (place < (g + 1) * piece)
        source_row = source_row + jnp.where(here, (assignment[me, g] - g) * piece + place, 0)
    chosen = (lax.broadcasted_iota(jnp.int32, (tok_rows, tok_rows), 1) == source_row)
    picked = jnp.dot(
        chosen.astype(jnp.float32).astype(jnp.bfloat16), q_all[...],
        preferred_element_type=jnp.float32,
    ).astype(jnp.bfloat16)
    for g in range(G):
        q_stage[g] = picked[g * piece:(g + 1) * piece]
    q_buf[me] = q_stage[me]
    pl.semaphore_wait(barrier, G - 1 + T - 1)

    def q_copy(i, source):
        return pltpu.make_async_remote_copy(
            src_ref=q_stage.at[lax.rem(me + i, G)], dst_ref=q_buf.at[source],
            send_sem=q_send.at[i], recv_sem=q_recv.at[i],
            device_id=(lax.rem(me + i, G), z), device_id_type=MESH,
        )

    def k_copy(i, source):
        return pltpu.make_async_remote_copy(
            src_ref=k_hbm.at[:, kv_cols], dst_ref=k_buf.at[source],
            send_sem=k_send.at[i], recv_sem=k_recv.at[i],
            device_id=(lax.rem(me + i, G), z), device_id_type=MESH,
        )

    def v_copy(i, source):
        return pltpu.make_async_remote_copy(
            src_ref=v_hbm.at[:, kv_cols], dst_ref=v_buf.at[source],
            send_sem=v_send.at[i], recv_sem=v_recv.at[i],
            device_id=(lax.rem(me + i, G), z), device_id_type=MESH,
        )

    for copy in (q_copy, k_copy, v_copy):
        for i in range(1, G):
            copy(i, me).start()
    own_k.wait()
    own_v.wait()
    for copy in (q_copy, k_copy, v_copy):
        for i in range(1, G):
            copy(i, lax.rem(me + G - i, G)).wait_recv()

    factor = HD ** (-0.5) * math.log2(math.e)

    def attend(s):
        span = (s + 1) * tok_rows
        q_rows = q_buf[s]
        if piece % 16:
            q_rows = q_rows.astype(jnp.float32)
        rows = jnp.concatenate(
            [q_rows[:, h * HD:(h + 1) * HD] for h in range(heads_here)], axis=0
        ).astype(jnp.bfloat16)
        keys = k_buf[:s + 1].reshape(span, HD)
        vals = v_buf[:s + 1].reshape(span, HD)
        q_pos = (
            s * tok_rows + assignment[s, me] * piece
            + lax.broadcasted_iota(jnp.int32, (piece, 1), 0)
        )
        start = jnp.zeros((piece, 1), jnp.int32)
        end = jnp.int32(0)
        for n in range(lengths.shape[0]):
            end = end + lengths[n]
            start = jnp.where(q_pos >= end, end, start)
        k_pos = lax.broadcasted_iota(jnp.int32, (piece, span), 1)
        bias = jnp.where((k_pos <= q_pos) & (k_pos >= start), 0.0, -1e30)
        scores = lax.dot_general(
            rows, keys, (((1,), (1,)), ((), ())), preferred_element_type=jnp.float32
        )
        scores = scores.reshape(heads_here, piece, span) * factor + bias[None]
        highest = jnp.max(scores, axis=2, keepdims=True)
        weights = jnp.exp2(scores - highest)
        total = jnp.sum(weights, axis=2, keepdims=True)
        summed = jnp.dot(
            weights.reshape(heads_here * piece, span).astype(jnp.bfloat16), vals,
            preferred_element_type=jnp.float32,
        ).reshape(heads_here, piece, HD)
        result = (summed / total).astype(att.dtype)
        for h in range(heads_here):
            att[s * piece:(s + 1) * piece, h * HD:(h + 1) * HD] = result[h]

    def product(t, c):
        rows = att[pl.ds(pl.multiple_of(t * out_rows, out_rows), out_rows), :]
        cols = w_buf[:, pl.ds(pl.multiple_of(c * cw, cw), cw)]
        return jnp.dot(rows.astype(jnp.bfloat16), cols, preferred_element_type=jnp.float32)

    def r_copy(k):
        return pltpu.make_async_remote_copy(
            src_ref=out_r.at[k], dst_ref=in_r.at[k],
            send_sem=r_send.at[k], recv_sem=r_recv.at[k],
            device_id=(me, lax.rem(z + 1, T)), device_id_type=MESH,
        )

    def l_copy(k):
        return pltpu.make_async_remote_copy(
            src_ref=out_l.at[k], dst_ref=in_l.at[k],
            send_sem=l_send.at[k], recv_sem=l_recv.at[k],
            device_id=(me, lax.rem(z + T - 1, T)), device_id_type=MESH,
        )

    def step(k, carry):
        c = k % CHUNKS
        t_r = T - 1 - k // CHUNKS
        t_l = k // CHUNKS

        @pl.when(z < t_r)
        def _():
            out_r[k] = product(t_r, c).astype(jnp.bfloat16)

            @pl.when(z > 0)
            def _():
                r_copy(k).wait_recv()
                out_r[k] = (
                    out_r[k].astype(jnp.float32) + in_r[k].astype(jnp.float32)
                ).astype(jnp.bfloat16)

            r_copy(k).start()

        @pl.when(z > t_l)
        def _():
            out_l[k] = product(t_l, c).astype(jnp.bfloat16)

            @pl.when(z < T - 1)
            def _():
                l_copy(k).wait_recv()
                out_l[k] = (
                    out_l[k].astype(jnp.float32) + in_l[k].astype(jnp.float32)
                ).astype(jnp.bfloat16)

            l_copy(k).start()

        return carry

    early = list(range(G - per_dest, G)) + list(range(per_dest))
    for s in early:
        attend(s)
    load_w.wait()
    lax.fori_loop(0, CHUNKS, step, 0)
    for s in range(G):
        if s not in early:
            attend(s)
    lax.fori_loop(CHUNKS, (T - 1) * CHUNKS, step, 0)

    def finish(c, carry):
        cols = pl.ds(pl.multiple_of(c * cw, cw), cw)
        out_ref[:, cols] = product(z, c).astype(jnp.bfloat16)

        @pl.when(z < T - 1)
        def _():
            k = z * CHUNKS + c
            l_copy(k).wait_recv()
            out_ref[:, cols] = (
                out_ref[:, cols].astype(jnp.float32) + in_l[k].astype(jnp.float32)
            ).astype(jnp.bfloat16)

        @pl.when(z > 0)
        def _():
            k = (T - 1 - z) * CHUNKS + c
            r_copy(k).wait_recv()
            out_ref[:, cols] = (
                out_ref[:, cols].astype(jnp.float32) + in_r[k].astype(jnp.float32)
            ).astype(jnp.bfloat16)

        return carry

    lax.fori_loop(0, CHUNKS, finish, 0)

    for copy in (q_copy, k_copy, v_copy):
        for i in range(1, G):
            copy(i, me).wait_send()

    def drain(k, carry):
        @pl.when(z < T - 1 - k // CHUNKS)
        def _():
            r_copy(k).wait_send()

        @pl.when(z > k // CHUNKS)
        def _():
            l_copy(k).wait_send()

        return carry

    lax.fori_loop(0, (T - 1) * CHUNKS, drain, 0)


def local(queries, keys, values, lengths, assignment, out_weight):
    G = lax.axis_size("dp")
    T = lax.axis_size("tensor")
    tok_rows, q_width = queries.shape
    n_cols = out_weight.shape[1]
    piece = tok_rows // G
    out_rows = tok_rows // T
    cw = n_cols // CHUNKS
    slots = (T - 1) * CHUNKS
    att_type = jnp.bfloat16 if piece % 16 == 0 else jnp.float32
    smem = pl.BlockSpec(memory_space=pltpu.SMEM)
    hbm = pl.BlockSpec(memory_space=pl.ANY)
    dma = pltpu.SemaphoreType.DMA
    bf16 = jnp.bfloat16

    def body(*refs):
        kernel(G, T, *refs)

    return pl.pallas_call(
        body,
        out_shape=jax.ShapeDtypeStruct((out_rows, n_cols), bf16),
        in_specs=[smem, smem, hbm, hbm, hbm, hbm],
        out_specs=pl.BlockSpec(memory_space=pltpu.VMEM),
        scratch_shapes=[
            pltpu.VMEM((tok_rows, q_width), bf16),
            pltpu.VMEM((G, piece, q_width), bf16),
            pltpu.VMEM((G, piece, q_width), bf16),
            pltpu.VMEM((G, tok_rows, HD), bf16),
            pltpu.VMEM((G, tok_rows, HD), bf16),
            pltpu.VMEM(out_weight.shape, bf16),
            pltpu.VMEM((tok_rows, q_width), att_type),
            pltpu.VMEM((slots, out_rows, cw), bf16),
            pltpu.VMEM((slots, out_rows, cw), bf16),
            pltpu.VMEM((slots, out_rows, cw), bf16),
            pltpu.VMEM((slots, out_rows, cw), bf16),
            dma, dma, dma((2,)),
            dma((G,)), dma((G,)), dma((G,)), dma((G,)), dma((G,)), dma((G,)),
            dma((slots,)), dma((slots,)), dma((slots,)), dma((slots,)),
        ],
        compiler_params=pltpu.CompilerParams(
            collective_id=0, has_side_effects=True, vmem_limit_bytes=60 << 20
        ),
    )(lengths, assignment, queries, keys, values, out_weight)


def solution(mesh):
    in_specs = (P("dp", "tensor"), P("dp", None), P("dp", None), P(), P(), P("tensor", None))
    out_specs = P(("dp", "tensor"), None)
    return jax.shard_map(local, mesh=mesh, in_specs=in_specs, out_specs=out_specs, check_vma=False)
```

time: 155 us -> 113 us (0.73)
  Pallas kernels: 0 us -> 109 us
  waiting for transfers between devices: 60.2 us -> 0 us
  blocking collectives: 20.1 us -> 0 us
  local copies, waits for them, and re-layouts: 20.3 us -> 2.06 us
  matrix products: 16.5 us -> 0 us
  between operations: 13.5 us -> 0.01 us
  other arithmetic: 11.7 us -> 0 us
  loops' own time: 6.67 us -> 0 us
  starting transfers between devices: 3.76 us -> 0 us
    pallas_call x0 -> x1, Pallas kernels: none -> 109 us  [local(): pl.pallas_call(body, out_shape=jax.ShapeDtypeStruct((out_rows, n_cols), b...]
    reduce_scatter x1 -> x0, waiting for transfers between devices: 60.1 us -> none  [local(): lax.psum_scatter(jnp.dot(attended, out_weight, preferred_element_type=jnp...]
    all_gather x2 -> x0, blocking collectives: 20.1 us -> none  [the longest x1 10.3 us: local(): k_rows = lax.all_gather(own_keys, 'dp', axis=0, tiled=True)]
    gather x10 -> x0, local copies, waits for them, and re-layouts: 16.8 us -> none  [the longest x8 13.8 us: attend(): k_doc = doc_all[jnp.clip(k_pos, 0, all_rows - 1)]]
    dot_general x17 -> x0, matrix products: 16.5 us -> none  [the longest x1 7.77 us: local(): jnp.dot(attended, out_weight, preferred_element_type=jnp.float32)]
    reduce_or x8 -> x0, other arithmetic: 7.09 us -> none  [attend(): return lax.cond(jnp.any(visible), compute, keep, softmax_state)]
    another operation x9 -> x0, loops' own time: 6.67 us -> none  [the longest x1 6.07 us: local(): lax.fori_loop(0, block_count, one_step, (running, totals, weighted))]
    all_to_all x1 -> x0, starting transfers between devices: 3.72 us -> none  [local(): lax.all_to_all(outgoing, 'dp', split_axis=0, concat_axis=0, tiled=True)]
  transfers between devices with their start and end apart: 2 -> 0, of which waited for: 1 -> 0; matrix products, arithmetic and copies ran while one was open for 3% -> 0% of each run, Pallas kernels for 0% -> 0%
where the time goes in v1:
time: 113 us; the launch traced here: 111 us
  Pallas kernels  109 us (96%)
  local copies, waits for them, and re-layouts  2.06 us (2%)
    pallas_call x1, Pallas kernels, local(): pl.pallas_call(body, out_shape=jax.ShapeDtypeStruct((out_rows, n_cols), b...  109 us

profile of v1, /device:TPU:8, one launch (start us, length us, event | category | flops | bytes accessed | tf_op | source)
XLA Modules:
  0.0 111.2 jit_solution(10450547052531316118)
XLA Ops:
  0.0 109.2 %shard_map.64 = bf16[64,6144]{1,0:T(8,128)(2,1)} custom-call(s32[4]{0:T(128)} %refs_0_.1, s32[8,8]{1,0:T(8,128)} %refs_1_.1, bf16[256,768]{1,0:T(8,128)(2,1)} %refs_2_.1, bf16[256,512]{1,0:T(8,128)(2,1)} %refs_3_.1, bf16[256,512]{1,0:T(8,128)(2,1)} %refs_4_.1, bf16[768,6144]{1,0:T(8,128)(2,1)} %refs_5_.1), custom_call_target="tpu_custom_call" | custom-call | tf_op jit(solution)/shard_map/pallas_call | solution.py:258
  109.2 2.1 %copy.8 = bf16[64,6144]{1,0:T(8,128)(2,1)} copy(bf16[64,6144]{1,0:T(8,128)(2,1)} %shard_map.64) | data formatting | bytes 1572864

commit v2 on v1

--- a/solution.py
+++ b/solution.py
@@ -152,14 +152,13 @@
             device_id=(me, lax.rem(z + T - 1, T)), device_id_type=MESH,
         )
 
-    def step(k, carry):
+    def right(k):
         c = k % CHUNKS
-        t_r = T - 1 - k // CHUNKS
-        t_l = k // CHUNKS
-
-        @pl.when(z < t_r)
-        def _():
-            out_r[k] = product(t_r, c).astype(jnp.bfloat16)
+        t = T - 1 - k // CHUNKS
+
+        @pl.when(z < t)
+        def _():
+            out_r[k] = product(t, c).astype(jnp.bfloat16)
 
             @pl.when(z > 0)
             def _():
@@ -170,9 +169,13 @@
 
             r_copy(k).start()
 
-        @pl.when(z > t_l)
-        def _():
-            out_l[k] = product(t_l, c).astype(jnp.bfloat16)
+    def left(k):
+        c = k % CHUNKS
+        t = k // CHUNKS
+
+        @pl.when(z > t)
+        def _():
+            out_l[k] = product(t, c).astype(jnp.bfloat16)
 
             @pl.when(z < T - 1)
             def _():
@@ -182,6 +185,17 @@
                 ).astype(jnp.bfloat16)
 
             l_copy(k).start()
+
+    def step(k, carry):
+        @pl.when(z < T // 2)
+        def _():
+            right(k)
+            left(k)
+
+        @pl.when(z >= T // 2)
+        def _():
+            left(k)
+            right(k)
 
         return carry
 

time: 113 us -> 83.2 us (0.74); the launches traced: 111 us -> 83 us
  Pallas kernels: 109 us -> 81 us
    pallas_call x1, Pallas kernels: 109 us -> 81 us  [local(): pl.pallas_call(body, out_shape=jax.ShapeDtypeStruct((out_rows, n_cols), b...]
where the time goes in v2:
time: 83.2 us; the launch traced here: 83 us
  Pallas kernels  81 us (97%)
  local copies, waits for them, and re-layouts  2.06 us (2%)
    pallas_call x1, Pallas kernels, local(): pl.pallas_call(body, out_shape=jax.ShapeDtypeStruct((out_rows, n_cols), b...  81 us
    unnamed x1, local copies, waits for them, and re-layouts  2.06 us

profile of v2, /device:TPU:8, one launch (start us, length us, event | category | flops | bytes accessed | tf_op | source)
XLA Modules:
  0.0 83.0 jit_solution(2941381557475656349)
XLA Ops:
  0.0 81.0 %shard_map.64 = bf16[64,6144]{1,0:T(8,128)(2,1)} custom-call(s32[4]{0:T(128)} %refs_0_.1, s32[8,8]{1,0:T(8,128)} %refs_1_.1, bf16[256,768]{1,0:T(8,128)(2,1)} %refs_2_.1, bf16[256,512]{1,0:T(8,128)(2,1)} %refs_3_.1, bf16[256,512]{1,0:T(8,128)(2,1)} %refs_4_.1, bf16[768,6144]{1,0:T(8,128)(2,1)} %refs_5_.1), custom_call_target="tpu_custom_call" | custom-call | tf_op jit(solution)/shard_map/pallas_call | solution.py:272
  81.0 2.1 %copy.8 = bf16[64,6144]{1,0:T(8,128)(2,1)} copy(bf16[64,6144]{1,0:T(8,128)(2,1)} %shard_map.64) | data formatting | bytes 1572864

commit v3 on v2

--- a/solution.py
+++ b/solution.py
@@ -19,6 +19,7 @@
     q_all, q_stage, q_buf, k_buf, v_buf, w_buf, att, in_r, in_l, out_r, out_l,
     load_sem, w_sem, own_sem, k_send, k_recv, v_send, v_recv, q_send, q_recv,
     r_send, r_recv, l_send, l_recv,
+    w_far, att_far, far_send, far_recv, near_send, near_recv, row_send, row_recv,
 ):
     me = lax.axis_index("dp")
     z = lax.axis_index("tensor")
@@ -29,6 +30,13 @@
     out_rows = tok_rows // T
     n_cols = w_buf.shape[1]
     cw = n_cols // CHUNKS
+    early_chunks = CHUNKS // 2
+    half = (T - 1) * early_chunks
+    parts, far_rows, far_cols = w_far.shape
+    share_rows = far_rows * parts // G
+    low, high = z == 0, z == T - 1
+    next_low, next_high = z == 1, z == T - 2
+    partner = me + 1 - 2 * (me % 2)
     kv_head = z * heads_here // (HEADS // KV_HEADS)
     kv_cols = pl.ds(pl.multiple_of(kv_head * HD, HD), HD)
 
@@ -86,6 +94,46 @@
             device_id=(lax.rem(me + i, G), z), device_id_type=MESH,
         )
 
+    def share(j):
+        rows = pl.ds(pl.multiple_of((j // parts) * share_rows, share_rows), share_rows)
+        return w_far.at[j % parts, rows, :]
+
+    def far_copy():
+        rows = pl.ds(pl.multiple_of((me // parts) * share_rows, share_rows), share_rows)
+        first = early_chunks * cw + (me % parts) * far_cols
+        cols = pl.ds(pl.multiple_of(first, far_cols), far_cols)
+        return pltpu.make_async_remote_copy(
+            src_ref=w_hbm.at[rows, cols], dst_ref=share(me),
+            send_sem=far_send, recv_sem=far_recv,
+            device_id=(me, jnp.where(z == 0, 1, T - 2)), device_id_type=MESH,
+        )
+
+    def peer_copy(i, owner):
+        return pltpu.make_async_remote_copy(
+            src_ref=share(owner), dst_ref=share(owner),
+            send_sem=near_send.at[i], recv_sem=near_recv.at[i],
+            device_id=(lax.rem(me + 2 * i, G), z), device_id_type=MESH,
+        )
+
+    def pass_copy(i, owner):
+        return pltpu.make_async_remote_copy(
+            src_ref=share(owner), dst_ref=share(owner),
+            send_sem=near_send.at[G // 2 + i], recv_sem=near_recv.at[G // 2 + i],
+            device_id=(partner, z), device_id_type=MESH,
+        )
+
+    def row_copy(t):
+        rows = pl.ds(t * out_rows, out_rows)
+        return pltpu.make_async_remote_copy(
+            src_ref=att.at[rows, :], dst_ref=att_far.at[rows, :],
+            send_sem=row_send.at[t], recv_sem=row_recv.at[t],
+            device_id=(me, jnp.where(z == 0, 1, T - 2)), device_id_type=MESH,
+        )
+
+    @pl.when(low | high)
+    def _():
+        far_copy().start()
+
     for copy in (q_copy, k_copy, v_copy):
         for i in range(1, G):
             copy(i, me).start()
@@ -94,6 +142,13 @@
     for copy in (q_copy, k_copy, v_copy):
         for i in range(1, G):
             copy(i, lax.rem(me + G - i, G)).wait_recv()
+
+    @pl.when(next_low | next_high)
+    def _():
+        far_copy().wait_recv()
+        for i in range(1, G // 2):
+            peer_copy(i, me).start()
+        pass_copy(0, me).start()
 
     factor = HD ** (-0.5) * math.log2(math.e)
 
@@ -152,37 +207,63 @@
             device_id=(me, lax.rem(z + T - 1, T)), device_id_type=MESH,
         )
 
+    def far_product(t, c):
+        rows = att_far[pl.ds(pl.multiple_of(t * out_rows, out_rows), out_rows), :]
+        rows = rows.astype(jnp.bfloat16)
+        per_chunk = cw // far_cols
+        return jnp.concatenate(
+            [
+                jnp.dot(
+                    rows, w_far[(c - early_chunks) * per_chunk + n],
+                    preferred_element_type=jnp.float32,
+                )
+                for n in range(per_chunk)
+            ],
+            axis=1,
+        )
+
+    def add_to(ref, index, more):
+        ref[index] = (ref[index].astype(jnp.float32) + more).astype(jnp.bfloat16)
+
+    def place_of(k):
+        return k % half // early_chunks, k // half * early_chunks + k % early_chunks
+
     def right(k):
-        c = k % CHUNKS
-        t = T - 1 - k // CHUNKS
-
-        @pl.when(z < t)
+        n, c = place_of(k)
+        t = T - 1 - n
+        late = k >= half
+
+        @pl.when((z < t) & ((z > 0) | (k < half)))
         def _():
             out_r[k] = product(t, c).astype(jnp.bfloat16)
 
-            @pl.when(z > 0)
+            @pl.when((z > 1) | ((z == 1) & (k < half)))
             def _():
                 r_copy(k).wait_recv()
-                out_r[k] = (
-                    out_r[k].astype(jnp.float32) + in_r[k].astype(jnp.float32)
-                ).astype(jnp.bfloat16)
+                add_to(out_r, k, in_r[k].astype(jnp.float32))
+
+            @pl.when((z == 1) & late)
+            def _():
+                add_to(out_r, k, far_product(t, c))
 
             r_copy(k).start()
 
     def left(k):
-        c = k % CHUNKS
-        t = k // CHUNKS
-
-        @pl.when(z > t)
+        t, c = place_of(k)
+        late = k >= half
+
+        @pl.when((z > t) & ((z < T - 1) | (k < half)))
         def _():
             out_l[k] = product(t, c).astype(jnp.bfloat16)
 
-            @pl.when(z < T - 1)
+            @pl.when((z < T - 2) | ((z == T - 2) & (k < half)))
             def _():
                 l_copy(k).wait_recv()
-                out_l[k] = (
-                    out_l[k].astype(jnp.float32) + in_l[k].astype(jnp.float32)
-                ).astype(jnp.bfloat16)
+                add_to(out_l, k, in_l[k].astype(jnp.float32))
+
+            @pl.when((z == T - 2) & late)
+            def _():
+                add_to(out_l, k, far_product(t, c))
 
             l_copy(k).start()
 
@@ -199,35 +280,69 @@
 
         return carry
 
-    early = list(range(G - per_dest, G)) + list(range(per_dest))
-    for s in early:
-        attend(s)
+    def send_rows(t):
+        @pl.when((low & (t > 0)) | (high & (t < T - 1)))
+        def _():
+            row_copy(t).start()
+
+    early = (T - 1, 0)
+    for t in early:
+        for s in range(t * per_dest, (t + 1) * per_dest):
+            attend(s)
     load_w.wait()
-    lax.fori_loop(0, CHUNKS, step, 0)
-    for s in range(G):
-        if s not in early:
-            attend(s)
-    lax.fori_loop(CHUNKS, (T - 1) * CHUNKS, step, 0)
+    lax.fori_loop(0, early_chunks, step, 0)
+    for t in range(T):
+        if t not in early:
+            for s in range(t * per_dest, (t + 1) * per_dest):
+                attend(s)
+
+    @pl.when(next_low | next_high)
+    def _():
+        for i in range(1, G // 2):
+            owner = lax.rem(me + G - 2 * i, G)
+            peer_copy(i, owner).wait_recv()
+            pass_copy(i, owner).start()
+
+    for t in range(T):
+        send_rows(t)
+    lax.fori_loop(early_chunks, half, step, 0)
+
+    @pl.when(next_low | next_high)
+    def _():
+        for i in range(G // 2):
+            pass_copy(i, lax.rem(partner + G - 2 * i, G)).wait_recv()
+        for t in range(T):
+            @pl.when((next_low & (t > 0)) | (next_high & (t < T - 1)))
+            def _():
+                row_copy(t).wait_recv()
+
+    lax.fori_loop(half, 2 * half, step, 0)
 
     def finish(c, carry):
         cols = pl.ds(pl.multiple_of(c * cw, cw), cw)
+        late = c >= early_chunks
+        base = c // early_chunks * half + c % early_chunks
+
+        def add_out(more):
+            out_ref[:, cols] = (out_ref[:, cols].astype(jnp.float32) + more).astype(jnp.bfloat16)
+
         out_ref[:, cols] = product(z, c).astype(jnp.bfloat16)
 
-        @pl.when(z < T - 1)
-        def _():
-            k = z * CHUNKS + c
+        @pl.when((next_low | next_high) & late)
+        def _():
+            add_out(far_product(z, c))
+
+        @pl.when((z < T - 2) | ((z == T - 2) & (c < early_chunks)))
+        def _():
+            k = base + z * early_chunks
             l_copy(k).wait_recv()
-            out_ref[:, cols] = (
-                out_ref[:, cols].astype(jnp.float32) + in_l[k].astype(jnp.float32)
-            ).astype(jnp.bfloat16)
-
-        @pl.when(z > 0)
-        def _():
-            k = (T - 1 - z) * CHUNKS + c
+            add_out(in_l[k].astype(jnp.float32))
+
+        @pl.when((z > 1) | ((z == 1) & (c < early_chunks)))
+        def _():
+            k = base + (T - 1 - z) * early_chunks
             r_copy(k).wait_recv()
-            out_ref[:, cols] = (
-                out_ref[:, cols].astype(jnp.float32) + in_r[k].astype(jnp.float32)
-            ).astype(jnp.bfloat16)
+            add_out(in_r[k].astype(jnp.float32))
 
         return carry
 
@@ -237,18 +352,35 @@
         for i in range(1, G):
             copy(i, me).wait_send()
 
+    @pl.when(low | high)
+    def _():
+        far_copy().wait_send()
+        for t in range(T):
+            @pl.when((low & (t > 0)) | (high & (t < T - 1)))
+            def _():
+                row_copy(t).wait_send()
+
+    @pl.when(next_low | next_high)
+    def _():
+        for i in range(1, G // 2):
+            peer_copy(i, me).wait_send()
+        for i in range(G // 2):
+            pass_copy(i, lax.rem(me + G - 2 * i, G)).wait_send()
+
     def drain(k, carry):
-        @pl.when(z < T - 1 - k // CHUNKS)
+        n, _ = place_of(k)
+
+        @pl.when((z < T - 1 - n) & ((z > 0) | (k < half)))
         def _():
             r_copy(k).wait_send()
 
-        @pl.when(z > k // CHUNKS)
+        @pl.when((z > n) & ((z < T - 1) | (k < half)))
         def _():
             l_copy(k).wait_send()
 
         return carry
 
-    lax.fori_loop(0, (T - 1) * CHUNKS, drain, 0)
+    lax.fori_loop(0, 2 * half, drain, 0)
 
 
 def local(queries, keys, values, lengths, assignment, out_weight):
@@ -260,6 +392,8 @@
     out_rows = tok_rows // T
     cw = n_cols // CHUNKS
     slots = (T - 1) * CHUNKS
+    parts = CHUNKS
+    far_cols = CHUNKS // 2 * cw // parts
     att_type = jnp.bfloat16 if piece % 16 == 0 else jnp.float32
     smem = pl.BlockSpec(memory_space=pltpu.SMEM)
     hbm = pl.BlockSpec(memory_space=pl.ANY)
@@ -289,6 +423,9 @@
             dma, dma, dma((2,)),
             dma((G,)), dma((G,)), dma((G,)), dma((G,)), dma((G,)), dma((G,)),
             dma((slots,)), dma((slots,)), dma((slots,)), dma((slots,)),
+            pltpu.VMEM((parts, q_width, far_cols), bf16),
+            pltpu.VMEM((tok_rows, q_width), att_type),
+            dma, dma, dma((G,)), dma((G,)), dma((T,)), dma((T,)),
         ],
         compiler_params=pltpu.CompilerParams(
             collective_id=0, has_side_effects=True, vmem_limit_bytes=60 << 20

time: 83.2 us -> 88.5 us (1.064)
  Pallas kernels: 81 us -> 85.5 us
    pallas_call x1, Pallas kernels: 81 us -> 85.5 us  [local(): pl.pallas_call(body, out_shape=jax.ShapeDtypeStruct((out_rows, n_cols), b...]
where the time goes in v3:
time: 88.5 us; the launch traced here: 87.6 us
  Pallas kernels  85.5 us (97%)
  local copies, waits for them, and re-layouts  2.06 us (2%)
    pallas_call x1, Pallas kernels, local(): pl.pallas_call(body, out_shape=jax.ShapeDtypeStruct((out_rows, n_cols), b...  85.5 us
    unnamed x1, local copies, waits for them, and re-layouts  2.06 us

profile of v3, /device:TPU:8, one launch (start us, length us, event | category | flops | bytes accessed | tf_op | source)
XLA Modules:
  0.0 87.6 jit_solution(789404057489574958)
XLA Ops:
  0.0 85.5 %shard_map.64 = bf16[64,6144]{1,0:T(8,128)(2,1)} custom-call(s32[4]{0:T(128)} %refs_0_.1, s32[8,8]{1,0:T(8,128)} %refs_1_.1, bf16[256,768]{1,0:T(8,128)(2,1)} %refs_2_.1, bf16[256,512]{1,0:T(8,128)(2,1)} %refs_3_.1, bf16[256,512]{1,0:T(8,128)(2,1)} %refs_4_.1, bf16[768,6144]{1,0:T(8,128)(2,1)} %refs_5_.1), custom_call_target="tpu_custom_call" | custom-call | tf_op jit(solution)/shard_map/pallas_call | solution.py:406
  85.5 2.1 %copy.8 = bf16[64,6144]{1,0:T(8,128)(2,1)} copy(bf16[64,6144]{1,0:T(8,128)(2,1)} %shard_map.64) | data formatting | bytes 1572864

commit v4 on v3

--- a/solution.py
+++ b/solution.py
@@ -12,6 +12,7 @@
 KV_HEADS = 4
 MESH = pl.DeviceIdType.MESH
 CHUNKS = 8
+LAG = 3
 
 
 def kernel(
@@ -80,19 +81,23 @@
             device_id=(lax.rem(me + i, G), z), device_id_type=MESH,
         )
 
-    def k_copy(i, source):
-        return pltpu.make_async_remote_copy(
-            src_ref=k_hbm.at[:, kv_cols], dst_ref=k_buf.at[source],
-            send_sem=k_send.at[i], recv_sem=k_recv.at[i],
-            device_id=(lax.rem(me + i, G), z), device_id_type=MESH,
-        )
-
-    def v_copy(i, source):
-        return pltpu.make_async_remote_copy(
-            src_ref=v_hbm.at[:, kv_cols], dst_ref=v_buf.at[source],
-            send_sem=v_send.at[i], recv_sem=v_recv.at[i],
-            device_id=(lax.rem(me + i, G), z), device_id_type=MESH,
-        )
+    def once_copy(which, i, source):
+        hbm, buf, send, recv = which
+        return pltpu.make_async_remote_copy(
+            src_ref=hbm.at[:, kv_cols], dst_ref=buf.at[source],
+            send_sem=send.at[i], recv_sem=recv.at[i],
+            device_id=(lax.rem(me + 2 * i, G), z), device_id_type=MESH,
+        )
+
+    def partner_copy(which, i, source):
+        hbm, buf, send, recv = which
+        return pltpu.make_async_remote_copy(
+            src_ref=hbm.at[:, kv_cols] if i == 0 else buf.at[source], dst_ref=buf.at[source],
+            send_sem=send.at[G // 2 + i], recv_sem=recv.at[G // 2 + i],
+            device_id=(partner, z), device_id_type=MESH,
+        )
+
+    both = ((k_hbm, k_buf, k_send, k_recv), (v_hbm, v_buf, v_send, v_recv))
 
     def share(j):
         rows = pl.ds(pl.multiple_of((j // parts) * share_rows, share_rows), share_rows)
@@ -134,14 +139,25 @@
     def _():
         far_copy().start()
 
-    for copy in (q_copy, k_copy, v_copy):
-        for i in range(1, G):
-            copy(i, me).start()
+    for which in both:
+        for i in range(1, G // 2):
+            once_copy(which, i, me).start()
+    for which in both:
+        partner_copy(which, 0, me).start()
+    for i in range(1, G):
+        q_copy(i, me).start()
     own_k.wait()
     own_v.wait()
-    for copy in (q_copy, k_copy, v_copy):
-        for i in range(1, G):
-            copy(i, lax.rem(me + G - i, G)).wait_recv()
+    for which in both:
+        for i in range(1, G // 2):
+            source = lax.rem(me + G - 2 * i, G)
+            once_copy(which, i, source).wait_recv()
+            partner_copy(which, i, source).start()
+    for which in both:
+        for i in range(G // 2):
+            partner_copy(which, i, lax.rem(partner + G - 2 * i, G)).wait_recv()
+    for i in range(1, G):
+        q_copy(i, lax.rem(me + G - i, G)).wait_recv()
 
     @pl.when(next_low | next_high)
     def _():
@@ -268,15 +284,28 @@
             l_copy(k).start()
 
     def step(k, carry):
+        k_r = k - LAG * jnp.maximum(z - 1, 0)
+        k_l = k - LAG * jnp.maximum(T - 2 - z, 0)
+
+        def go_right():
+            @pl.when((k_r >= 0) & (k_r < 2 * half))
+            def _():
+                right(k_r)
+
+        def go_left():
+            @pl.when((k_l >= 0) & (k_l < 2 * half))
+            def _():
+                left(k_l)
+
         @pl.when(z < T // 2)
         def _():
-            right(k)
-            left(k)
+            go_right()
+            go_left()
 
         @pl.when(z >= T // 2)
         def _():
-            left(k)
-            right(k)
+            go_left()
+            go_right()
 
         return carry
 
@@ -316,7 +345,7 @@
             def _():
                 row_copy(t).wait_recv()
 
-    lax.fori_loop(half, 2 * half, step, 0)
+    lax.fori_loop(half, 2 * half + LAG * (T - 2), step, 0)
 
     def finish(c, carry):
         cols = pl.ds(pl.multiple_of(c * cw, cw), cw)
@@ -348,9 +377,13 @@
 
     lax.fori_loop(0, CHUNKS, finish, 0)
 
-    for copy in (q_copy, k_copy, v_copy):
-        for i in range(1, G):
-            copy(i, me).wait_send()
+    for i in range(1, G):
+        q_copy(i, me).wait_send()
+    for which in both:
+        for i in range(1, G // 2):
+            once_copy(which, i, me).wait_send()
+        for i in range(G // 2):
+            partner_copy(which, i, me).wait_send()
 
     @pl.when(low | high)
     def _():

time: 88.5 us -> 78.3 us (0.88)
  Pallas kernels: 85.5 us -> 76 us
    pallas_call x1, Pallas kernels: 85.5 us -> 76 us  [local(): pl.pallas_call(body, out_shape=jax.ShapeDtypeStruct((out_rows, n_cols), b...]
where the time goes in v4:
time: 78.3 us; the launch traced here: 78.1 us
  Pallas kernels  76 us (97%)
  local copies, waits for them, and re-layouts  2.06 us (3%)
    pallas_call x1, Pallas kernels, local(): pl.pallas_call(body, out_shape=jax.ShapeDtypeStruct((out_rows, n_cols), b...  76 us
    unnamed x1, local copies, waits for them, and re-layouts  2.06 us

profile of v4, /device:TPU:8, one launch (start us, length us, event | category | flops | bytes accessed | tf_op | source)
XLA Modules:
  0.0 78.1 jit_solution(1732206871189846683)
XLA Ops:
  0.0 76.0 %shard_map.64 = bf16[64,6144]{1,0:T(8,128)(2,1)} custom-call(s32[4]{0:T(128)} %refs_0_.1, s32[8,8]{1,0:T(8,128)} %refs_1_.1, bf16[256,768]{1,0:T(8,128)(2,1)} %refs_2_.1, bf16[256,512]{1,0:T(8,128)(2,1)} %refs_3_.1, bf16[256,512]{1,0:T(8,128)(2,1)} %refs_4_.1, bf16[768,6144]{1,0:T(8,128)(2,1)} %refs_5_.1), custom_call_target="tpu_custom_call" | custom-call | tf_op jit(solution)/shard_map/pallas_call | solution.py:439
  76.0 2.1 %copy.8 = bf16[64,6144]{1,0:T(8,128)(2,1)} copy(bf16[64,6144]{1,0:T(8,128)(2,1)} %shard_map.64) | data formatting | bytes 1572864

commit v5 on v4

--- a/solution.py
+++ b/solution.py
@@ -325,16 +325,16 @@
             for s in range(t * per_dest, (t + 1) * per_dest):
                 attend(s)
 
+    for t in range(T):
+        send_rows(t)
+    lax.fori_loop(early_chunks, half, step, 0)
+
     @pl.when(next_low | next_high)
     def _():
         for i in range(1, G // 2):
             owner = lax.rem(me + G - 2 * i, G)
             peer_copy(i, owner).wait_recv()
             pass_copy(i, owner).start()
-
-    for t in range(T):
-        send_rows(t)
-    lax.fori_loop(early_chunks, half, step, 0)
 
     @pl.when(next_low | next_high)
     def _():

time: 78.3 us -> 73.2 us (0.935)
  Pallas kernels: 76 us -> 70.8 us
    pallas_call x1, Pallas kernels: 76 us -> 70.8 us  [local(): pl.pallas_call(body, out_shape=jax.ShapeDtypeStruct((out_rows, n_cols), b...]
where the time goes in v5:
time: 73.2 us; the launch traced here: 72.8 us
  Pallas kernels  70.8 us (97%)
  local copies, waits for them, and re-layouts  2.06 us (3%)
    pallas_call x1, Pallas kernels, local(): pl.pallas_call(body, out_shape=jax.ShapeDtypeStruct((out_rows, n_cols), b...  70.8 us
    unnamed x1, local copies, waits for them, and re-layouts  2.06 us

profile of v5, /device:TPU:8, one launch (start us, length us, event | category | flops | bytes accessed | tf_op | source)
XLA Modules:
  0.0 72.8 jit_solution(14359113095998458191)
XLA Ops:
  0.0 70.8 %shard_map.64 = bf16[64,6144]{1,0:T(8,128)(2,1)} custom-call(s32[4]{0:T(128)} %refs_0_.1, s32[8,8]{1,0:T(8,128)} %refs_1_.1, bf16[256,768]{1,0:T(8,128)(2,1)} %refs_2_.1, bf16[256,512]{1,0:T(8,128)(2,1)} %refs_3_.1, bf16[256,512]{1,0:T(8,128)(2,1)} %refs_4_.1, bf16[768,6144]{1,0:T(8,128)(2,1)} %refs_5_.1), custom_call_target="tpu_custom_call" | custom-call | tf_op jit(solution)/shard_map/pallas_call | solution.py:439
  70.8 2.1 %copy.8 = bf16[64,6144]{1,0:T(8,128)(2,1)} copy(bf16[64,6144]{1,0:T(8,128)(2,1)} %shard_map.64) | data formatting | bytes 1572864

commit v6 on v5

--- a/solution.py
+++ b/solution.py
@@ -327,7 +327,36 @@
 
     for t in range(T):
         send_rows(t)
+    def finish(c, carry):
+        cols = pl.ds(pl.multiple_of(c * cw, cw), cw)
+        late = c >= early_chunks
+        base = c // early_chunks * half + c % early_chunks
+
+        def add_out(more):
+            out_ref[:, cols] = (out_ref[:, cols].astype(jnp.float32) + more).astype(jnp.bfloat16)
+
+        out_ref[:, cols] = product(z, c).astype(jnp.bfloat16)
+
+        @pl.when((next_low | next_high) & late)
+        def _():
+            add_out(far_product(z, c))
+
+        @pl.when((z < T - 2) | ((z == T - 2) & (c < early_chunks)))
+        def _():
+            k = base + z * early_chunks
+            l_copy(k).wait_recv()
+            add_out(in_l[k].astype(jnp.float32))
+
+        @pl.when((z > 1) | ((z == 1) & (c < early_chunks)))
+        def _():
+            k = base + (T - 1 - z) * early_chunks
+            r_copy(k).wait_recv()
+            add_out(in_r[k].astype(jnp.float32))
+
+        return carry
+
     lax.fori_loop(early_chunks, half, step, 0)
+    lax.fori_loop(0, early_chunks, finish, 0)
 
     @pl.when(next_low | next_high)
     def _():
@@ -347,35 +376,7 @@
 
     lax.fori_loop(half, 2 * half + LAG * (T - 2), step, 0)
 
-    def finish(c, carry):
-        cols = pl.ds(pl.multiple_of(c * cw, cw), cw)
-        late = c >= early_chunks
-        base = c // early_chunks * half + c % early_chunks
-
-        def add_out(more):
-            out_ref[:, cols] = (out_ref[:, cols].astype(jnp.float32) + more).astype(jnp.bfloat16)
-
-        out_ref[:, cols] = product(z, c).astype(jnp.bfloat16)
-
-        @pl.when((next_low | next_high) & late)
-        def _():
-            add_out(far_product(z, c))
-
-        @pl.when((z < T - 2) | ((z == T - 2) & (c < early_chunks)))
-        def _():
-            k = base + z * early_chunks
-            l_copy(k).wait_recv()
-            add_out(in_l[k].astype(jnp.float32))
-
-        @pl.when((z > 1) | ((z == 1) & (c < early_chunks)))
-        def _():
-            k = base + (T - 1 - z) * early_chunks
-            r_copy(k).wait_recv()
-            add_out(in_r[k].astype(jnp.float32))
-
-        return carry
-
-    lax.fori_loop(0, CHUNKS, finish, 0)
+    lax.fori_loop(early_chunks, CHUNKS, finish, 0)
 
     for i in range(1, G):
         q_copy(i, me).wait_send()

time: 73.2 us -> 80.4 us (1.098)
  Pallas kernels: 70.8 us -> 77.9 us
    pallas_call x1, Pallas kernels: 70.8 us -> 77.9 us  [local(): pl.pallas_call(body, out_shape=jax.ShapeDtypeStruct((out_rows, n_cols), b...]
where the time goes in v6:
time: 80.4 us; the launch traced here: 79.9 us
  Pallas kernels  77.9 us (97%)
  local copies, waits for them, and re-layouts  2.06 us (3%)
    pallas_call x1, Pallas kernels, local(): pl.pallas_call(body, out_shape=jax.ShapeDtypeStruct((out_rows, n_cols), b...  77.9 us
    unnamed x1, local copies, waits for them, and re-layouts  2.06 us

profile of v6, /device:TPU:8, one launch (start us, length us, event | category | flops | bytes accessed | tf_op | source)
XLA Modules:
  0.0 79.9 jit_solution(6955214954322881578)
XLA Ops:
  0.0 77.9 %shard_map.64 = bf16[64,6144]{1,0:T(8,128)(2,1)} custom-call(s32[4]{0:T(128)} %refs_0_.1, s32[8,8]{1,0:T(8,128)} %refs_1_.1, bf16[256,768]{1,0:T(8,128)(2,1)} %refs_2_.1, bf16[256,512]{1,0:T(8,128)(2,1)} %refs_3_.1, bf16[256,512]{1,0:T(8,128)(2,1)} %refs_4_.1, bf16[768,6144]{1,0:T(8,128)(2,1)} %refs_5_.1), custom_call_target="tpu_custom_call" | custom-call | tf_op jit(solution)/shard_map/pallas_call | solution.py:440
  77.9 2.1 %copy.8 = bf16[64,6144]{1,0:T(8,128)(2,1)} copy(bf16[64,6144]{1,0:T(8,128)(2,1)} %shard_map.64) | data formatting | bytes 1572864
